TPU v7x, 32 devices: a whole 2x2x4 slice. The times are simulated.
32 devices in a mesh: seq: 4 (over y, core), shard: 8 (over z, x).
Axes of the slice: x: 2, y: 2, z: 4, core: 2. Of those that a mesh axis runs over, the one named last changes fastest.
Arguments:
- hidden_in: bfloat16 [8, 1024, 1024], P('shard', 'seq'), may hold values from -6 to 6
- norm_gain: float32 [1024], replicated, may hold values from 0.5 to 1.5
- in_weight: bfloat16 [1024, 4384], P('shard'), may hold values from -0.1875 to 0.1875
- conv_weight: float32 [4, 2304], replicated, may hold values from -3 to 3
- conv_bias: float32 [2304], replicated, may hold values from -0.5 to 0.5
- dt_bias: float32 [32], replicated, may hold values from -4 to -1
- a_log: float32 [32], replicated, may hold values from -6 to 1
- skip: float32 [32], replicated, may hold values from 0.5 to 1.5
- inner_gain: float32 [2048], replicated, may hold values from 0.5 to 1.5
- out_weight: bfloat16 [2048, 1024], P('shard'), may hold values from -0.125 to 0.125
- out_grad: float32 [8, 1024, 1024], P('shard', 'seq'), may hold values from -6 to 6
Outputs:
- block_out: float32 [8, 1024, 1024], P('shard', 'seq')
- input_grad: float32 [8, 1024, 1024], P('shard', 'seq')
- norm_gain_grad: float32 [1024], replicated
- in_weight_grad: float32 [1024, 4384], P('shard')
- conv_weight_grad: float32 [4, 2304], replicated
- conv_bias_grad: float32 [2304], replicated
- dt_bias_grad: float32 [32], replicated
- a_log_grad: float32 [32], replicated
- skip_grad: float32 [32], replicated
- inner_gain_grad: float32 [2048], replicated
- out_weight_grad: float32 [2048, 1024], P('shard')
All inputs are finite; a program needn't handle non-finite values.
Results may differ from a plain program's by a relative error of at most 0.015.
Values may be sent and summed in bfloat16 or wider, within the bound.
No kernel may reach another device: no remote copies, remote signals or barrier semaphores. Data moves between devices by JAX's collectives and lax.ppermute only.
A program may use at most 128 MiB of HBM per device.

v0:
```python
import jax
import jax.numpy as jnp
from jax import lax
from jax.sharding import PartitionSpec as P

STATE = 128
GROUP = 256
norm_eps = 1e-05
highest = lax.Precision.HIGHEST


def passed_along(block, axis, distance):
    devices = range(lax.axis_size(axis))
    route = [(i - distance, i) for i in devices if i - distance in devices]
    return lax.ppermute(block, axis, route)


def contract_rows(left, right):
    return lax.dot_general(
        left, right, (((0,), (0,)), ((), ())), preferred_element_type=jnp.float32
    )


def contract_cols(left, right):
    return lax.dot_general(
        left, right, (((1,), (1,)), ((), ())), preferred_element_type=jnp.float32
    )


def section_one(conv_ext, dt_raw, conv_weight, conv_bias, dt_bias, a_log):
    rows = dt_raw.shape[0]
    width = conv_weight.shape[0]
    conv_out = conv_bias + conv_weight[0] * conv_ext[0:rows]
    for offset in range(1, width):
        conv_out = conv_out + conv_weight[offset] * conv_ext[offset : offset + rows]
    active = jax.nn.silu(conv_out)
    inner = conv_out.shape[1] - 2 * STATE
    x_heads = active[:, :inner]
    b_proj = active[:, inner : inner + STATE]
    c_proj = active[:, inner + STATE :]
    step_size = jax.nn.softplus(dt_raw + dt_bias)
    log_decay = -step_size * jnp.exp(a_log)
    return (x_heads, b_proj, c_proj, step_size, log_decay)


def ssd_groups(x_heads, b_proj, c_proj, step_size, log_decay, h_start):
    rows, heads = step_size.shape
    head_dim = x_heads.shape[1] // heads
    state_dim = b_proj.shape[1]
    blocks = rows // GROUP
    lower = jnp.arange(GROUP)[:, None] >= jnp.arange(GROUP)[None, :]
    mask = lower[None, :, :]

    def ssd_advance(state, pieces):
        x_blk, b_blk, c_blk, dt_blk, ld_blk = pieces
        cumul = jnp.cumsum(ld_blk, axis=0)
        cum_t = cumul.T
        spread = cum_t[:, :, None] - cum_t[:, None, :]
        kernel = jnp.where(mask, jnp.exp(jnp.where(mask, spread, 0.0)), 0.0)
        intersection = jnp.dot(c_blk, b_blk.T, precision=highest)
        kernel = kernel * intersection[None, :, :] * dt_blk.T[:, None, :]
        output = jnp.einsum("hts,shp->thp", kernel, x_blk, precision=highest)
        output = output + jnp.exp(cumul)[:, :, None] * jnp.einsum(
            "hpn,tn->thp", state, c_blk, precision=highest
        )
        weight_tail = jnp.exp(cumul[-1][None, :] - cumul) * dt_blk
        fresh = jnp.einsum("sh,shp,sn->hpn", weight_tail, x_blk, b_blk, precision=highest)
        state = jnp.exp(cumul[-1])[:, None, None] * state + fresh
        return (state, output)

    pieces = (
        x_heads.reshape(blocks, GROUP, heads, head_dim),
        b_proj.reshape(blocks, GROUP, state_dim),
        c_proj.reshape(blocks, GROUP, state_dim),
        step_size.reshape(blocks, GROUP, heads),
        log_decay.reshape(blocks, GROUP, heads),
    )
    h_end, outputs = lax.scan(ssd_advance, h_start, pieces)
    return (outputs.reshape(rows, heads * head_dim), h_end)


def end_states(x_heads, b_proj, step_size, log_decay, h_start):
    rows, heads = step_size.shape
    head_dim = x_heads.shape[1] // heads
    state_dim = b_proj.shape[1]
    blocks = rows // GROUP

    def end_advance(state, pieces):
        x_blk, b_blk, dt_blk, ld_blk = pieces
        cumul = jnp.cumsum(ld_blk, axis=0)
        weight_tail = jnp.exp(cumul[-1][None, :] - cumul) * dt_blk
        fresh = jnp.einsum("sh,shp,sn->hpn", weight_tail, x_blk, b_blk, precision=highest)
        return (jnp.exp(cumul[-1])[:, None, None] * state + fresh, None)

    pieces = (
        x_heads.reshape(blocks, GROUP, heads, head_dim),
        b_proj.reshape(blocks, GROUP, state_dim),
        step_size.reshape(blocks, GROUP, heads),
        log_decay.reshape(blocks, GROUP, heads),
    )
    h_end, unused = lax.scan(end_advance, h_start, pieces)
    return h_end


def section_three(ssd_out, x_heads, gate_z, skip, inner_gain):
    rows = ssd_out.shape[0]
    heads = skip.shape[0]
    mixed = ssd_out + (x_heads.reshape(rows, heads, -1) * skip[None, :, None]).reshape(rows, -1)
    gated_in = mixed * jax.nn.silu(gate_z)
    scale = lax.rsqrt(jnp.mean(gated_in * gated_in, axis=-1, keepdims=True) + norm_eps)
    return gated_in * scale * inner_gain


def body(
    hidden_in,
    norm_gain,
    in_weight,
    conv_weight,
    conv_bias,
    dt_bias,
    a_log,
    skip,
    inner_gain,
    out_weight,
    out_grad,
):
    tokens = hidden_in[0]
    tokens_f = tokens.astype(jnp.float32)
    cotan = out_grad[0]
    inner = inner_gain.shape[0]
    conv_dim = conv_bias.shape[0]
    width = conv_weight.shape[0]
    heads = dt_bias.shape[0]
    head_dim = inner // heads
    rows = tokens.shape[0]
    edge = rows - (width - 1)
    full_in, full_out = (
        lax.all_gather(in_weight, "shard", axis=0, tiled=True),
        lax.all_gather(out_weight, "shard", axis=0, tiled=True),
    )
    rstat = lax.rsqrt(jnp.mean(tokens_f * tokens_f, axis=-1, keepdims=True) + norm_eps)
    normed = (tokens_f * rstat * norm_gain).astype(jnp.bfloat16)
    projected = jnp.dot(normed, full_in, preferred_element_type=jnp.float32)
    gate_z = projected[:, :inner]
    conv_in = projected[:, inner : inner + conv_dim].astype(jnp.bfloat16)
    dt_raw = projected[:, inner + conv_dim :]
    before = passed_along(conv_in[edge:], "seq", 1)
    conv_ext = jnp.concatenate([before, conv_in], axis=0).astype(jnp.float32)
    firsts, back_one = jax.vjp(
        section_one, conv_ext, dt_raw, conv_weight, conv_bias, dt_bias, a_log
    )
    x_heads, b_proj, c_proj, step_size, log_decay = firsts
    h_zero = jnp.zeros((heads, head_dim, b_proj.shape[1]), jnp.float32)
    local_state = end_states(x_heads, b_proj, step_size, log_decay, h_zero)
    passing = jnp.exp(jnp.sum(log_decay, axis=0))

    def relay_step(turn, incoming):
        return passed_along(passing[:, None, None] * incoming + local_state, "seq", 1)

    h_in = lax.fori_loop(0, lax.axis_size("seq") - 1, relay_step, h_zero)

    def scan_states(x_one, b_one, c_one, s_one, l_one):
        return ssd_groups(x_one, b_one, c_one, s_one, l_one, h_in)

    (ssd_out, unused), back_two = jax.vjp(
        scan_states, x_heads, b_proj, c_proj, step_size, log_decay
    )
    growth = jnp.exp(jnp.cumsum(log_decay, axis=0))
    gated_pre, back_three = jax.vjp(section_three, ssd_out, x_heads, gate_z, skip, inner_gain)
    gated = gated_pre.astype(jnp.bfloat16)
    block_out = tokens_f + jnp.dot(gated, full_out, preferred_element_type=jnp.float32)
    cot_b = cotan.astype(jnp.bfloat16)
    d_gated = contract_cols(cot_b, lax.all_gather(out_weight, "shard", axis=0, tiled=True))
    d_ssd, d_x_three, d_gate, skip_grad, inner_gain_grad = back_three(d_gated)
    d_heads = d_ssd.reshape(rows, heads, head_dim)
    pulled = jnp.einsum("th,thp,tn->hpn", growth, d_heads, c_proj, precision=highest)

    def back_step(turn, later):
        return passed_along(
            (pulled + passing[:, None, None] * later).astype(jnp.bfloat16), "seq", -1
        ).astype(jnp.float32)

    h_grad = lax.fori_loop(0, lax.axis_size("seq") - 1, back_step, h_zero)
    d_x_two, d_b, d_c, d_step, d_log = back_two((d_ssd, h_grad))
    d_ext, d_dt_raw, conv_weight_part, conv_bias_part, dt_bias_part, a_log_part = back_one(
        (d_x_two + d_x_three, d_b, d_c, d_step, d_log)
    )
    returned = passed_along(d_ext[: width - 1], "seq", -1)
    d_conv = d_ext[width - 1 :]
    d_conv = jnp.concatenate([d_conv[:edge], d_conv[edge:] + returned], axis=0)
    d_proj = jnp.concatenate([d_gate, d_conv, d_dt_raw], axis=1).astype(jnp.bfloat16)
    d_normed = contract_cols(d_proj, lax.all_gather(in_weight, "shard", axis=0, tiled=True))
    norm_part = jnp.sum(d_normed * tokens_f * rstat, axis=0)
    scaled = norm_gain * d_normed
    input_grad = (
        cotan
        + rstat * scaled
        - tokens_f * rstat * rstat * rstat * jnp.mean(scaled * tokens_f, axis=-1, keepdims=True)
    )
    in_share = lax.psum_scatter(
        contract_rows(normed, d_proj).astype(jnp.bfloat16), "shard", scatter_dimension=0, tiled=True
    )
    out_share = lax.psum_scatter(
        contract_rows(gated, cot_b).astype(jnp.bfloat16), "shard", scatter_dimension=0, tiled=True
    )
    in_weight_grad, out_weight_grad = (
        lax.psum(in_share, "seq").astype(jnp.float32),
        lax.psum(out_share, "seq").astype(jnp.float32),
    )
    smalls = lax.psum(
        (
            norm_part,
            conv_weight_part,
            conv_bias_part,
            dt_bias_part,
            a_log_part,
            skip_grad,
            inner_gain_grad,
        ),
        ("seq", "shard"),
    )
    (
        norm_gain_grad,
        conv_weight_grad,
        conv_bias_grad,
        dt_bias_grad,
        a_log_grad,
        skip_total,
        gain_total,
    ) = smalls
    return (
        block_out[None],
        input_grad[None],
        norm_gain_grad,
        in_weight_grad,
        conv_weight_grad,
        conv_bias_grad,
        dt_bias_grad,
        a_log_grad,
        skip_total,
        gain_total,
        out_weight_grad,
    )


def solution(mesh):
    placed = (
        P("shard", "seq", None),
        P(),
        P("shard", None),
        P(),
        P(),
        P(),
        P(),
        P(),
        P(),
        P("shard", None),
        P("shard", "seq", None),
    )
    return jax.shard_map(
        body,
        mesh=mesh,
        in_specs=placed,
        out_specs=(
            P("shard", "seq", None),
            P("shard", "seq", None),
            P(),
            P("shard", None),
            P(),
            P(),
            P(),
            P(),
            P(),
            P(),
            P("shard", None),
        ),
        check_vma=False,
    )
```

profile of v0, /device:TPU:0, one launch (start us, length us, event | category | flops | bytes accessed | tf_op | source)
XLA Modules:
  0.0 726.6 jit_solution(14364811259111382184)
XLA Ops:
  13.8 131.1 %all-gather.3.cloned.1.call-done = bf16[1024,4384]{0,1:T(8,128)(2,1)} async-done(((bf16[128,4384]{0,1:T(8,128)(2,1)}), bf16[1024,4384]{0,1:T(8,128)(2,1)}) %all-gather.3.cloned.1.call-update) | async-done | bytes 8978448 | tf_op jit(solution)/shard_map/all_gather | solution.py:138
  144.9 6.3 fusion.107
  172.7 4.4 fusion.40
  177.2 43.8 %while.17 = (s32[]{:T(128)}, f32[32,64,128]{2,1,0:T(8,128)S(1)}, f32[32]{0:T(128)S(1)}, f32[32,64,128]{2,1,0:T(8,128)}, s32[]{:T(128)}) while((s32[]{:T(128)}, f32[32,64,128]{2,1,0:T(8,128)S(1)}, f32[32]{0:T(128)S(1)}, f32[32,64,128]{2,1,0:T(8,128)}, s32[]{:T(128)}) %tuple.98), condition=%wide.region_5.6_spmd, body=%wide.region_4.5_spmd.sunk | while | flops 524290 | bytes 7340261 | solution.py:160
  179.6 3.9 collective-permute-start
  188.3 11.5 %collective-permute-start = (f32[32,64,128]{2,1,0:T(8,128)}, f32[32,64,128]{2,1,0:T(8,128)S(1)}, u32[]{:S(2)}, u32[]{:S(2)}) collective-permute-start(f32[32,64,128]{2,1,0:T(8,128)} %multiply_add_fusion.7), channel_id=1, source_target_pairs={{0,8},{8,16},{16,24},{1,9},{9,17},{17,25},{2,10},{10,18},{18,26},{... | collective-permute-start | bytes 3145736 | tf_op jit(solution)/shard_map/while/body/eval_jaxpr/ppermute | solution.py:15
  204.6 13.9 %collective-permute-start = (f32[32,64,128]{2,1,0:T(8,128)}, f32[32,64,128]{2,1,0:T(8,128)S(1)}, u32[]{:S(2)}, u32[]{:S(2)}) collective-permute-start(f32[32,64,128]{2,1,0:T(8,128)} %multiply_add_fusion.7), channel_id=1, source_target_pairs={{0,8},{8,16},{16,24},{1,9},{9,17},{17,25},{2,10},{10,18},{18,26},{... | collective-permute-start | bytes 3145736 | tf_op jit(solution)/shard_map/while/body/eval_jaxpr/ppermute | solution.py:15
  223.9 11.9 %bitcast_add_fusion.1 = f32[256,32,64]{0,2,1:T(8,128)} fusion(f32[256,32,64]{0,2,1:T(8,128)S(1)} %fusion.78, f32[256,32,64]{0,2,1:T(8,128)S(1)} %bitcast.138, f32[32,256]{1,0:T(8,128)S(1)} %copy-done.48, f32[256,256]{1,0:T(8,128)S(1)} %copy-done.29, f32[32,256]{1,0:T(8,128)S(1)} %copy-done.50, pred[256,256]{1,0:T(8,128)(4,1)S(1)} %copy-done.44, ...), kind=kOutput, calls=%fused_computation.48 | convolution fusion | flops 1622147072 | bytes 6717440 | tf_op jit(solution)/shard_map/jvp()/while/body/eval_jaxpr/hts,shp->thp/dot_general | solution.py:62
  239.0 4.9 multiply_reduce_fusion.11
  245.0 5.6 multiply_reduce_fusion.7
  250.7 4.6 multiply_reduce_fusion.8
  258.3 3.4 multiply_reduce_fusion.9
  261.7 3.7 fusion.29
  265.4 51.5 %while.18 = (s32[]{:T(128)}, f32[32,64,128]{2,1,0:T(8,128)}, f32[32]{0:T(128)}, f32[32,64,128]{2,1,0:T(8,128)}, s32[]{:T(128)}, /*index=5*/s32[]{:T(128)}) while((s32[]{:T(128)}, f32[32,64,128]{2,1,0:T(8,128)}, f32[32]{0:T(128)}, f32[32,64,128]{2,1,0:T(8,128)}, s32[]{:T(128)}, /*index=5*/s32[]{:T(128)}) %tuple.115), condition=%wide.region_10.11_spmd.clone, body=%wide.region_9.10_spmd.clone.sunk | while | flops 1310723 | bytes 6291703 | solution.py:183
  268.9 14.3 %collective-permute-done.1 = bf16[32,64,128]{2,1,0:T(8,128)(2,1)} collective-permute-done((bf16[32,64,128]{2,1,0:T(8,128)(2,1)}, bf16[32,64,128]{2,1,0:T(8,128)(2,1)}, u32[]{:S(2)}, u32[]{:S(2)}) %collective-permute-start.1) | collective-permute-done | bytes 524320 | tf_op jit(solution)/shard_map/while/body/eval_jaxpr/ppermute | solution.py:15
  289.2 10.2 %collective-permute-done.1 = bf16[32,64,128]{2,1,0:T(8,128)(2,1)} collective-permute-done((bf16[32,64,128]{2,1,0:T(8,128)(2,1)}, bf16[32,64,128]{2,1,0:T(8,128)(2,1)}, u32[]{:S(2)}, u32[]{:S(2)}) %collective-permute-start.1) | collective-permute-done | bytes 524320 | tf_op jit(solution)/shard_map/while/body/eval_jaxpr/ppermute | solution.py:15
  305.3 9.5 %collective-permute-done.1 = bf16[32,64,128]{2,1,0:T(8,128)(2,1)} collective-permute-done((bf16[32,64,128]{2,1,0:T(8,128)(2,1)}, bf16[32,64,128]{2,1,0:T(8,128)(2,1)}, u32[]{:S(2)}, u32[]{:S(2)}) %collective-permute-start.1) | collective-permute-done | bytes 524320 | tf_op jit(solution)/shard_map/while/body/eval_jaxpr/ppermute | solution.py:15
  316.9 3.8 multiply_reduce_fusion.6
  322.4 4.1 fusion.46
  326.5 14.6 %fusion.10 = (f32[32,256]{1,0:T(8,128)}, f32[32,256]{1,0:T(8,128)}, f32[32,256]{1,0:T(8,128)}, f32[256,256]{1,0:T(8,128)}) fusion(f32[32,256]{1,0:T(8,128)S(1)} %copy-done.49, f32[256,256]{1,0:T(8,128)S(1)} %copy-done.30, f32[32,256]{1,0:T(8,128)S(1)} %copy-done.51, pred[256,256]{1,0:T(8,128)(4,1)S(1)} %copy-done.45, f32[32,64,256]{2,1,0:T(8,128)S(1)} %bitcast.142, ...), kind=kOutput, calls=%fused_computation.15 | convolution fusion | flops 1641979904 | bytes 4947968 | tf_op jit(solution)/shard_map/transpose(jvp())/while/body/eval_jaxpr/hts,shp->thp/dot_general | solution.py:62
  341.1 8.8 %bitcast_add_fusion = f32[256,32,64]{0,2,1:T(8,128)} fusion(f32[256,32,64]{0,2,1:T(8,128)S(1)} %get-tuple-element.505, f32[32,64,256]{2,1,0:T(8,128)S(1)} %bitcast.143, f32[32,256]{1,0:T(8,128)S(1)} %copy-done.49, f32[256,256]{1,0:T(8,128)S(1)} %copy-done.30, f32[32,256]{1,0:T(8,128)S(1)} %copy-done.51, pred[256,256]{1,0:T(8,128)(4,1)S(1)} %copy-done.45, ...), kind=kOutput, calls=%fused_computation.47 | convolution fusion | flops 1622147072 | bytes 6717440 | tf_op jit(solution)/shard_map/transpose(jvp())/while/body/eval_jaxpr/hts,shp->thp/dot_general | solution.py:62
  352.8 5.8 fusion.106
  361.5 5.2 convolution_bitcast_fusion
  387.6 5.8 collective-permute-done.3
  394.3 6.1 convolution_convert_fusion
  400.5 11.8 %copy.162 = bf16[1024,4384]{1,0:T(8,128)(2,1)} copy(bf16[1024,4384]{0,1:T(8,128)(2,1)} %convolution_convert_fusion) | data formatting | bytes 17956864
  414.1 3.4 convolution_convert_fusion.1
  418.4 4.7 fusion.43
  423.1 149.3 %reduce-scatter.7.cloned.1.call-done = bf16[128,4384]{1,0:T(8,128)(2,1)} async-done(((bf16[1024,4384]{1,0:T(8,128)(2,1)}), bf16[128,4384]{1,0:T(8,128)(2,1)}) %reduce-scatter.7.cloned.1.call-update) | async-done | bytes 1122320
  574.8 88.6 %reduce-scatter.5.cloned.1.call-done = bf16[256,1024]{1,0:T(8,128)(2,1)} async-done(((bf16[2048,1024]{1,0:T(8,128)(2,1)}), bf16[256,1024]{1,0:T(8,128)(2,1)}) %reduce-scatter.5.cloned.1.call-update) | async-done | bytes 524304 | tf_op jit(solution)/shard_map/reduce_scatter | solution.py:203
  663.4 7.6 %fusion.57 = (f32[1024]{0:T(1024)S(1)}, f32[256]{0:T(256)S(1)}, f32[256,1024]{1,0:T(8,128)}) fusion(bf16[1,256,1024]{2,1,0:T(8,128)(2,1)S(1)} %copy-done.23, f32[256]{0:T(256)S(1)} %copy-done.64, f32[1024]{0:T(1024)S(1)} %copy-done.57, bf16[1024,4384]{0,1:T(8,128)(2,1)} %all-gather.3.cloned.1.call-done, bf16[256,32]{1,0:T(8,128)(2,1)S(1)} %get-tuple-element.482, ...), kind=kOutput, calls=%fused_computation.92 | convolution fusion | flops 2309290752 | bytes 12806144 | tf_op jit(solution)/shard_map/dot_general | solution.py:25
  671.0 42.5 %all-reduce.13 = (f32[1024]{0:T(1024)}, f32[4,2304]{1,0:T(4,128)}, f32[2304]{0:T(1024)}, f32[32]{0:T(128)}, f32[32]{0:T(128)}, /*index=5*/f32[32]{0:T(128)}, f32[2048]{0:T(1024)}) all-reduce(f32[1024]{0:T(1024)S(1)} %get-tuple-element.448, f32[4,2304]{1,0:T(4,128)S(1)} %pad_add_fusion.2, ...), channel_id=1, replica_groups=mesh['seq'=4,'shard'=8] {'seq','shard'}, use_global_device_ids=true, to_apply=%region_21.22 | all-reduce | flops 14688 | bytes 117504 | tf_op jit(solution)/shard_map/psum | solution.py:210
  (251 shorter events, 110.6 us)
Async XLA Ops:
  7.2 137.8 %copy-start.21 = (bf16[1,256,1024]{2,1,0:T(8,128)(2,1)S(1)}, bf16[1,256,1024]{2,1,0:T(8,128)(2,1)}, u32[]{:S(2)}) copy-start(bf16[1,256,1024]{2,1,0:T(8,128)(2,1)} %param.15) | copy-start | bytes 1572868
  7.2 137.8 %copy-start.56 = (f32[1024]{0:T(1024)S(1)}, f32[1024]{0:T(1024)}, u32[]{:S(2)}) copy-start(f32[1024]{0:T(1024)} %param.16) | copy-start | bytes 12292
  7.2 137.7 %all-gather.3.cloned.1.call-start = ((), (), s32[]{:S(2)}) async-start(), calls=%async_computation.2 | async-start | bytes 10100736 | tf_op jit(solution)/shard_map/all_gather | solution.py:138
  7.9 237.0 %all-gather.5.cloned.1.call-start = ((), (), s32[]{:S(2)}) async-start(), calls=%async_computation.3 | async-start | bytes 4718592 | tf_op jit(solution)/shard_map/all_gather | solution.py:139
  8.7 563.7 %reduce-scatter.7.cloned.1.call-start = ((), (), s32[]{:S(2)}) async-start(), calls=%async_computation.5 | async-start | bytes 10321920
  9.4 143.3 %copy-start.67 = (f32[32]{0:T(128)}, f32[32]{0:T(128)S(1)}, u32[]{:S(2)}) copy-start(f32[32]{0:T(128)S(1)} %exp.120) | copy-start | bytes 388
  12.5 149.3 %copy-start.34 = (f32[2304]{0:T(1024)}, f32[2304]{0:T(1024)S(1)}, u32[]{:S(2)}) copy-start(f32[2304]{0:T(1024)S(1)} %get-tuple-element.450) | copy-start | bytes 27652
  12.5 149.3 %copy-start.36 = (f32[2304]{0:T(1024)}, f32[2304]{0:T(1024)S(1)}, u32[]{:S(2)}) copy-start(f32[2304]{0:T(1024)S(1)} %get-tuple-element.451) | copy-start | bytes 27652
  12.5 149.3 %copy-start.38 = (f32[2304]{0:T(1024)}, f32[2304]{0:T(1024)S(1)}, u32[]{:S(2)}) copy-start(f32[2304]{0:T(1024)S(1)} %get-tuple-element.452) | copy-start | bytes 27652
  12.5 149.3 %copy-start.40 = (f32[2304]{0:T(1024)}, f32[2304]{0:T(1024)S(1)}, u32[]{:S(2)}) copy-start(f32[2304]{0:T(1024)S(1)} %get-tuple-element.453) | copy-start | bytes 27652
  13.8 137.4 %copy-start.63 = (f32[256]{0:T(256)}, f32[256]{0:T(256)S(1)}, u32[]{:S(2)}) copy-start(f32[256]{0:T(256)S(1)} %add_rsqrt_fusion) | copy-start | bytes 3076
  13.8 139.5 %copy-start.58 = (f32[32]{0:T(128)S(1)}, f32[32]{0:T(128)}, u32[]{:S(2)}) copy-start(f32[32]{0:T(128)} %param.20) | copy-start | bytes 388
  151.2 9.0 %collective-permute-start.2 = (bf16[3,2304]{1,0:T(4,128)(2,1)S(1)}, bf16[3,2304]{1,0:T(4,128)(2,1)S(1)}, u32[]{:S(2)}, u32[]{:S(2)}) collective-permute-start(bf16[3,2304]{1,0:T(4,128)(2,1)S(1)} %slice.123), channel_id=1, source_target_pairs={{0,8},{8,16},{16,24},{1,9},{9,17},{17,25},{2,10},{10,18},{18,26},{... | collective-permute-start | bytes 41480 | tf_op jit(solution)/shard_map/ppermute | solution.py:15
  179.6 6.3 collective-permute-start
  188.3 13.9 %collective-permute-start = (f32[32,64,128]{2,1,0:T(8,128)}, f32[32,64,128]{2,1,0:T(8,128)S(1)}, u32[]{:S(2)}, u32[]{:S(2)}) collective-permute-start(f32[32,64,128]{2,1,0:T(8,128)} %multiply_add_fusion.7), channel_id=1, source_target_pairs={{0,8},{8,16},{16,24},{1,9},{9,17},{17,25},{2,10},{10,18},{18,26},{... | collective-permute-start | bytes 3145736 | tf_op jit(solution)/shard_map/while/body/eval_jaxpr/ppermute | solution.py:15
  204.6 16.3 %collective-permute-start = (f32[32,64,128]{2,1,0:T(8,128)}, f32[32,64,128]{2,1,0:T(8,128)S(1)}, u32[]{:S(2)}, u32[]{:S(2)}) collective-permute-start(f32[32,64,128]{2,1,0:T(8,128)} %multiply_add_fusion.7), channel_id=1, source_target_pairs={{0,8},{8,16},{16,24},{1,9},{9,17},{17,25},{2,10},{10,18},{18,26},{... | collective-permute-start | bytes 3145736 | tf_op jit(solution)/shard_map/while/body/eval_jaxpr/ppermute | solution.py:15
  220.9 14.9 %copy-start.46 = (f32[32]{0:T(128)}, f32[32]{0:T(128)S(1)}, u32[]{:S(2)}) copy-start(f32[32]{0:T(128)S(1)} %get-tuple-element.620) | copy-start | bytes 388
  223.9 11.9 %copy-start.17 = (f32[256,32,64]{0,2,1:T(8,128)}, f32[256,32,64]{0,2,1:T(8,128)S(1)}, u32[]{:S(2)}) copy-start(f32[256,32,64]{0,2,1:T(8,128)S(1)} %fusion.78) | copy-start | bytes 6291460
  267.6 15.6 %collective-permute-start.1 = (bf16[32,64,128]{2,1,0:T(8,128)(2,1)}, bf16[32,64,128]{2,1,0:T(8,128)(2,1)}, u32[]{:S(2)}, u32[]{:S(2)}) collective-permute-start(bf16[32,64,128]{2,1,0:T(8,128)(2,1)} %fusion.132), channel_id=1, source_target_pairs={{8,0},{16,8},{24,16},{9,1},{17,9},{25,17},{10,2},{18,10},{26,18},{... | collective-permute-start | bytes 1572872 | tf_op jit(solution)/shard_map/while/body/eval_jaxpr/ppermute | solution.py:15
  287.9 11.4 %collective-permute-start.1 = (bf16[32,64,128]{2,1,0:T(8,128)(2,1)}, bf16[32,64,128]{2,1,0:T(8,128)(2,1)}, u32[]{:S(2)}, u32[]{:S(2)}) collective-permute-start(bf16[32,64,128]{2,1,0:T(8,128)(2,1)} %fusion.132), channel_id=1, source_target_pairs={{8,0},{16,8},{24,16},{9,1},{17,9},{25,17},{10,2},{18,10},{26,18},{... | collective-permute-start | bytes 1572872 | tf_op jit(solution)/shard_map/while/body/eval_jaxpr/ppermute | solution.py:15
  304.0 10.8 %collective-permute-start.1 = (bf16[32,64,128]{2,1,0:T(8,128)(2,1)}, bf16[32,64,128]{2,1,0:T(8,128)(2,1)}, u32[]{:S(2)}, u32[]{:S(2)}) collective-permute-start(bf16[32,64,128]{2,1,0:T(8,128)(2,1)} %fusion.132), channel_id=1, source_target_pairs={{8,0},{16,8},{24,16},{9,1},{17,9},{25,17},{10,2},{18,10},{26,18},{... | collective-permute-start | bytes 1572872 | tf_op jit(solution)/shard_map/while/body/eval_jaxpr/ppermute | solution.py:15
  361.5 8.2 %copy-start.15 = (f32[256,2304]{1,0:T(8,128)S(1)}, f32[256,2304]{1,0:T(8,128)}, u32[]{:S(2)}) copy-start(f32[256,2304]{1,0:T(8,128)} %get-tuple-element.487) | copy-start | bytes 7077892
  361.5 8.2 %copy-start.18 = (f32[256,2048]{1,0:T(8,128)S(1)}, f32[256,2048]{1,0:T(8,128)}, u32[]{:S(2)}) copy-start(f32[256,2048]{1,0:T(8,128)} %get-tuple-element.499) | copy-start | bytes 6291460
  377.8 7.0 copy-start.68
  383.4 9.9 %copy-start.6 = (f32[256,2304]{1,0:T(8,128)S(1)}, f32[256,2304]{1,0:T(8,128)}, u32[]{:S(2)}) copy-start(f32[256,2304]{1,0:T(8,128)} %copy-done.5) | copy-start | bytes 7077892
  383.4 9.9 %collective-permute-start.3 = (f32[3,2304]{1,0:T(4,128)S(1)}, f32[3,2304]{1,0:T(4,128)S(1)}, u32[]{:S(2)}, u32[]{:S(2)}) collective-permute-start(f32[3,2304]{1,0:T(4,128)S(1)} %pad_add_fusion.1), channel_id=1, source_target_pairs={{8,0},{16,8},{24,16},{9,1},{17,9},{25,17},{10,2},{18,10},{26,18},{... | collective-permute-start | bytes 82952 | tf_op jit(solution)/shard_map/ppermute | solution.py:15
  387.5 6.8 copy-start.24
  412.3 251.1 %reduce-scatter.5.cloned.1.call-start = ((), (), s32[]{:S(2)}) async-start(), calls=%async_computation.4 | async-start | bytes 4718592 | tf_op jit(solution)/shard_map/reduce_scatter | solution.py:203
  417.5 298.5 %all-reduce.17.cloned.1.call-start = ((), (), s32[]{:S(2)}) async-start(), calls=%async_computation.6 | async-start | bytes 3293184 | tf_op jit(solution)/shard_map/psum | solution.py:207
  423.1 240.3 %copy-start.23 = (bf16[1,256,1024]{2,1,0:T(8,128)(2,1)S(1)}, bf16[1,256,1024]{2,1,0:T(8,128)(2,1)}, u32[]{:S(2)}) copy-start(bf16[1,256,1024]{2,1,0:T(8,128)(2,1)} %param.15) | copy-start | bytes 1572868
  423.1 240.3 %copy-start.25 = (bf16[253,2304]{1,0:T(8,128)(2,1)S(1)}, bf16[253,2304]{1,0:T(8,128)(2,1)}, u32[]{:S(2)}) copy-start(bf16[253,2304]{1,0:T(8,128)(2,1)} %copy-done.24) | copy-start | bytes 3497476
  663.4 7.6 %copy-start.55 = (f32[2048]{0:T(1024)S(1)}, f32[2048]{0:T(1024)}, u32[]{:S(2)}) copy-start(f32[2048]{0:T(1024)} %get-tuple-element.445) | copy-start | bytes 24580
  (52 other events, 180.5 us)
Sparse Core Ops, SparseCore 0:
  10.1 134.8 all-gather.2
  147.1 70.9 all-gather.4
  412.4 159.9 reduce-scatter.6
  575.9 87.3 reduce-scatter.4
  666.2 45.0 all-reduce.16
where the time goes:
time: 731 us; the launch traced here: 727 us
  waiting for transfers between devices  417 us (57%)
  matrix products  98 us (13%)
  other arithmetic  67.7 us (9%)
  local copies, waits for them, and re-layouts  49.9 us (7%)
  blocking collectives  42.5 us (6%)
  starting transfers between devices  36.2 us (5%)
  between operations  14.9 us (2%)
    unnamed x6, waiting for transfers between devices  151 us
    all_gather x1, waiting for transfers between devices, body(): lax.all_gather(in_weight, 'shard', axis=0, tiled=True)  131 us
    reduce_scatter x1, waiting for transfers between devices, body(): lax.psum_scatter(contract_rows(gated, cot_b).astype(jnp.bfloat16), 'shard...  88.6 us
    ppermute x8, waiting for transfers between devices, passed_along(): return lax.ppermute(block, axis, route)  46.9 us
    psum x1, blocking collectives, body(): lax.psum((norm_part, conv_weight_part, conv_bias_part, dt_bias_part, a_lo...  42.5 us
    ppermute x8, starting transfers between devices, passed_along(): return lax.ppermute(block, axis, route)  36 us
    dot_general x3, matrix products, ssd_advance(): output = jnp.einsum('hts,shp->thp', kernel, x_blk, precision=highest)  35.2 us
    unnamed x144, local copies, waits for them, and re-layouts  22.8 us
  transfers between devices with their start and end apart: 13, of which 10 were waited for; matrix products, arithmetic and copies ran while one was open for 12% of the time, Pallas kernels for 0%

commit v1 on v0

--- a/solution.py
+++ b/solution.py
@@ -207,18 +207,17 @@
         lax.psum(in_share, "seq").astype(jnp.float32),
         lax.psum(out_share, "seq").astype(jnp.float32),
     )
-    smalls = lax.psum(
-        (
-            norm_part,
-            conv_weight_part,
-            conv_bias_part,
-            dt_bias_part,
-            a_log_part,
-            skip_grad,
-            inner_gain_grad,
-        ),
-        ("seq", "shard"),
-    )
+    smalls = (
+        norm_part,
+        conv_weight_part,
+        conv_bias_part,
+        dt_bias_part,
+        a_log_part,
+        skip_grad,
+        inner_gain_grad,
+    )
+    for name in ("shard", "seq"):
+        smalls = lax.psum(smalls, name)
     (
         norm_gain_grad,
         conv_weight_grad,

time: 731 us -> 736 us (level)
    psum x1 -> x2, blocking collectives: 42.5 us -> 47.6 us  [body(): smalls = lax.psum(smalls, name)]
where the time goes in v1:
time: 736 us; the launch traced here: 732 us
  waiting for transfers between devices  417 us (57%)
  matrix products  98 us (13%)
  other arithmetic  67.7 us (9%)
  local copies, waits for them, and re-layouts  49.9 us (7%)
  blocking collectives  47.6 us (6%)
  starting transfers between devices  36.2 us (5%)
  between operations  14.9 us (2%)
    unnamed x6, waiting for transfers between devices  151 us
    all_gather x1, waiting for transfers between devices, body(): lax.all_gather(in_weight, 'shard', axis=0, tiled=True)  131 us
    reduce_scatter x1, waiting for transfers between devices, body(): lax.psum_scatter(contract_rows(gated, cot_b).astype(jnp.bfloat16), 'shard...  88.6 us
    psum x2, blocking collectives, body(): smalls = lax.psum(smalls, name)  47.6 us
    ppermute x8, waiting for transfers between devices, passed_along(): return lax.ppermute(block, axis, route)  46.9 us
    ppermute x8, starting transfers between devices, passed_along(): return lax.ppermute(block, axis, route)  36 us
    dot_general x3, matrix products, ssd_advance(): output = jnp.einsum('hts,shp->thp', kernel, x_blk, precision=highest)  35.2 us
    unnamed x144, local copies, waits for them, and re-layouts  22.8 us
  transfers between devices with their start and end apart: 13, of which 10 were waited for; matrix products, arithmetic and copies ran while one was open for 12% of the time, Pallas kernels for 0%

profile of v1, /device:TPU:0, one launch (start us, length us, event | category | flops | bytes accessed | tf_op | source)
XLA Modules:
  0.0 731.8 jit_solution(17844243235737477580)
XLA Ops:
  13.8 131.1 %all-gather.3.cloned.1.call-done = bf16[1024,4384]{0,1:T(8,128)(2,1)} async-done(((bf16[128,4384]{0,1:T(8,128)(2,1)}), bf16[1024,4384]{0,1:T(8,128)(2,1)}) %all-gather.3.cloned.1.call-update) | async-done | bytes 8978448 | tf_op jit(solution)/shard_map/all_gather | solution.py:138
  144.9 6.3 fusion.107
  172.7 4.4 fusion.40
  177.2 43.8 %while.17 = (s32[]{:T(128)}, f32[32,64,128]{2,1,0:T(8,128)S(1)}, f32[32]{0:T(128)S(1)}, f32[32,64,128]{2,1,0:T(8,128)}, s32[]{:T(128)}) while((s32[]{:T(128)}, f32[32,64,128]{2,1,0:T(8,128)S(1)}, f32[32]{0:T(128)S(1)}, f32[32,64,128]{2,1,0:T(8,128)}, s32[]{:T(128)}) %tuple.98), condition=%wide.region_5.6_spmd, body=%wide.region_4.5_spmd.sunk | while | flops 524290 | bytes 7340261 | solution.py:160
  179.6 3.9 collective-permute-start
  188.3 11.5 %collective-permute-start = (f32[32,64,128]{2,1,0:T(8,128)}, f32[32,64,128]{2,1,0:T(8,128)S(1)}, u32[]{:S(2)}, u32[]{:S(2)}) collective-permute-start(f32[32,64,128]{2,1,0:T(8,128)} %multiply_add_fusion.7), channel_id=1, source_target_pairs={{0,8},{8,16},{16,24},{1,9},{9,17},{17,25},{2,10},{10,18},{18,26},{... | collective-permute-start | bytes 3145736 | tf_op jit(solution)/shard_map/while/body/eval_jaxpr/ppermute | solution.py:15
  204.6 13.9 %collective-permute-start = (f32[32,64,128]{2,1,0:T(8,128)}, f32[32,64,128]{2,1,0:T(8,128)S(1)}, u32[]{:S(2)}, u32[]{:S(2)}) collective-permute-start(f32[32,64,128]{2,1,0:T(8,128)} %multiply_add_fusion.7), channel_id=1, source_target_pairs={{0,8},{8,16},{16,24},{1,9},{9,17},{17,25},{2,10},{10,18},{18,26},{... | collective-permute-start | bytes 3145736 | tf_op jit(solution)/shard_map/while/body/eval_jaxpr/ppermute | solution.py:15
  223.9 11.9 %bitcast_add_fusion.1 = f32[256,32,64]{0,2,1:T(8,128)} fusion(f32[256,32,64]{0,2,1:T(8,128)S(1)} %fusion.78, f32[256,32,64]{0,2,1:T(8,128)S(1)} %bitcast.138, f32[32,256]{1,0:T(8,128)S(1)} %copy-done.48, f32[256,256]{1,0:T(8,128)S(1)} %copy-done.29, f32[32,256]{1,0:T(8,128)S(1)} %copy-done.50, pred[256,256]{1,0:T(8,128)(4,1)S(1)} %copy-done.44, ...), kind=kOutput, calls=%fused_computation.48 | convolution fusion | flops 1622147072 | bytes 6717440 | tf_op jit(solution)/shard_map/jvp()/while/body/eval_jaxpr/hts,shp->thp/dot_general | solution.py:62
  239.0 4.9 multiply_reduce_fusion.11
  245.0 5.6 multiply_reduce_fusion.7
  250.7 4.6 multiply_reduce_fusion.8
  258.3 3.4 multiply_reduce_fusion.9
  261.7 3.7 fusion.29
  265.4 51.5 %while.18 = (s32[]{:T(128)}, f32[32,64,128]{2,1,0:T(8,128)}, f32[32]{0:T(128)}, f32[32,64,128]{2,1,0:T(8,128)}, s32[]{:T(128)}, /*index=5*/s32[]{:T(128)}) while((s32[]{:T(128)}, f32[32,64,128]{2,1,0:T(8,128)}, f32[32]{0:T(128)}, f32[32,64,128]{2,1,0:T(8,128)}, s32[]{:T(128)}, /*index=5*/s32[]{:T(128)}) %tuple.115), condition=%wide.region_10.11_spmd.clone, body=%wide.region_9.10_spmd.clone.sunk | while | flops 1310723 | bytes 6291703 | solution.py:183
  268.9 14.3 %collective-permute-done.1 = bf16[32,64,128]{2,1,0:T(8,128)(2,1)} collective-permute-done((bf16[32,64,128]{2,1,0:T(8,128)(2,1)}, bf16[32,64,128]{2,1,0:T(8,128)(2,1)}, u32[]{:S(2)}, u32[]{:S(2)}) %collective-permute-start.1) | collective-permute-done | bytes 524320 | tf_op jit(solution)/shard_map/while/body/eval_jaxpr/ppermute | solution.py:15
  289.2 10.2 %collective-permute-done.1 = bf16[32,64,128]{2,1,0:T(8,128)(2,1)} collective-permute-done((bf16[32,64,128]{2,1,0:T(8,128)(2,1)}, bf16[32,64,128]{2,1,0:T(8,128)(2,1)}, u32[]{:S(2)}, u32[]{:S(2)}) %collective-permute-start.1) | collective-permute-done | bytes 524320 | tf_op jit(solution)/shard_map/while/body/eval_jaxpr/ppermute | solution.py:15
  305.3 9.5 %collective-permute-done.1 = bf16[32,64,128]{2,1,0:T(8,128)(2,1)} collective-permute-done((bf16[32,64,128]{2,1,0:T(8,128)(2,1)}, bf16[32,64,128]{2,1,0:T(8,128)(2,1)}, u32[]{:S(2)}, u32[]{:S(2)}) %collective-permute-start.1) | collective-permute-done | bytes 524320 | tf_op jit(solution)/shard_map/while/body/eval_jaxpr/ppermute | solution.py:15
  316.9 3.8 multiply_reduce_fusion.6
  322.4 4.1 fusion.46
  326.5 14.6 %fusion.10 = (f32[32,256]{1,0:T(8,128)}, f32[32,256]{1,0:T(8,128)}, f32[32,256]{1,0:T(8,128)}, f32[256,256]{1,0:T(8,128)}) fusion(f32[32,256]{1,0:T(8,128)S(1)} %copy-done.49, f32[256,256]{1,0:T(8,128)S(1)} %copy-done.30, f32[32,256]{1,0:T(8,128)S(1)} %copy-done.51, pred[256,256]{1,0:T(8,128)(4,1)S(1)} %copy-done.45, f32[32,64,256]{2,1,0:T(8,128)S(1)} %bitcast.142, ...), kind=kOutput, calls=%fused_computation.15 | convolution fusion | flops 1641979904 | bytes 4947968 | tf_op jit(solution)/shard_map/transpose(jvp())/while/body/eval_jaxpr/hts,shp->thp/dot_general | solution.py:62
  341.1 8.8 %bitcast_add_fusion = f32[256,32,64]{0,2,1:T(8,128)} fusion(f32[256,32,64]{0,2,1:T(8,128)S(1)} %get-tuple-element.512, f32[32,64,256]{2,1,0:T(8,128)S(1)} %bitcast.143, f32[32,256]{1,0:T(8,128)S(1)} %copy-done.49, f32[256,256]{1,0:T(8,128)S(1)} %copy-done.30, f32[32,256]{1,0:T(8,128)S(1)} %copy-done.51, pred[256,256]{1,0:T(8,128)(4,1)S(1)} %copy-done.45, ...), kind=kOutput, calls=%fused_computation.47 | convolution fusion | flops 1622147072 | bytes 6717440 | tf_op jit(solution)/shard_map/transpose(jvp())/while/body/eval_jaxpr/hts,shp->thp/dot_general | solution.py:62
  352.8 5.8 fusion.106
  361.5 5.2 convolution_bitcast_fusion
  387.6 5.8 collective-permute-done.3
  394.3 6.1 convolution_convert_fusion
  400.5 11.8 %copy.162 = bf16[1024,4384]{1,0:T(8,128)(2,1)} copy(bf16[1024,4384]{0,1:T(8,128)(2,1)} %convolution_convert_fusion) | data formatting | bytes 17956864
  418.4 4.7 fusion.43
  423.1 149.3 %reduce-scatter.7.cloned.1.call-done = bf16[128,4384]{1,0:T(8,128)(2,1)} async-done(((bf16[1024,4384]{1,0:T(8,128)(2,1)}), bf16[128,4384]{1,0:T(8,128)(2,1)}) %reduce-scatter.7.cloned.1.call-update) | async-done | bytes 1122320
  574.8 88.6 %reduce-scatter.5.cloned.1.call-done = bf16[256,1024]{1,0:T(8,128)(2,1)} async-done(((bf16[2048,1024]{1,0:T(8,128)(2,1)}), bf16[256,1024]{1,0:T(8,128)(2,1)}) %reduce-scatter.5.cloned.1.call-update) | async-done | bytes 524304 | tf_op jit(solution)/shard_map/reduce_scatter | solution.py:203
  663.4 7.6 %fusion.57 = (f32[1024]{0:T(1024)S(1)}, f32[256]{0:T(256)S(1)}, f32[256,1024]{1,0:T(8,128)}) fusion(bf16[1,256,1024]{2,1,0:T(8,128)(2,1)S(1)} %copy-done.23, f32[256]{0:T(256)S(1)} %copy-done.64, f32[1024]{0:T(1024)S(1)} %copy-done.57, bf16[1024,4384]{0,1:T(8,128)(2,1)} %all-gather.3.cloned.1.call-done, bf16[256,32]{1,0:T(8,128)(2,1)S(1)} %get-tuple-element.489, ...), kind=kOutput, calls=%fused_computation.92 | convolution fusion | flops 2309290752 | bytes 12806144 | tf_op jit(solution)/shard_map/dot_general | solution.py:25
  671.0 36.3 %all-reduce.13 = (f32[1024]{0:T(1024)S(1)}, f32[4,2304]{1,0:T(4,128)S(1)}, f32[2304]{0:T(1024)S(1)}, f32[32]{0:T(128)S(1)}, f32[32]{0:T(128)S(1)}, /*index=5*/f32[32]{0:T(128)S(1)}, f32[2048]{0:T(1024)S(1)}) all-reduce(f32[1024]{0:T(1024)S(1)} %get-tuple-element.448, ...), channel_id=1, replica_groups=mesh['seq'=4,'shard'=8] {'shard'}, use_global_device_ids=true, to_apply=%region_21.22 | all-reduce | flops 14688 | bytes 117504 | tf_op jit(solution)/shard_map/psum | solution.py:220
  707.3 11.3 %all-reduce.14 = (f32[1024]{0:T(1024)}, f32[4,2304]{1,0:T(4,128)}, f32[2304]{0:T(1024)}, f32[32]{0:T(128)}, f32[32]{0:T(128)}, /*index=5*/f32[32]{0:T(128)}, f32[2048]{0:T(1024)}) all-reduce(f32[1024]{0:T(1024)S(1)} %get-tuple-element.470, f32[4,2304]{1,0:T(4,128)S(1)} %get-tuple-element.471, ...), channel_id=1, replica_groups=mesh['seq'=4,'shard'=8] {'seq'}, use_global_device_ids=true, to_apply=%region_22.23 | all-reduce | flops 14688 | bytes 117504 | tf_op jit(solution)/shard_map/psum | solution.py:220
  (252 shorter events, 114.0 us)
Async XLA Ops:
  7.2 137.8 %copy-start.21 = (bf16[1,256,1024]{2,1,0:T(8,128)(2,1)S(1)}, bf16[1,256,1024]{2,1,0:T(8,128)(2,1)}, u32[]{:S(2)}) copy-start(bf16[1,256,1024]{2,1,0:T(8,128)(2,1)} %param.15) | copy-start | bytes 1572868
  7.2 137.8 %copy-start.56 = (f32[1024]{0:T(1024)S(1)}, f32[1024]{0:T(1024)}, u32[]{:S(2)}) copy-start(f32[1024]{0:T(1024)} %param.16) | copy-start | bytes 12292
  7.2 137.7 %all-gather.3.cloned.1.call-start = ((), (), s32[]{:S(2)}) async-start(), calls=%async_computation.2 | async-start | bytes 10100736 | tf_op jit(solution)/shard_map/all_gather | solution.py:138
  7.9 237.0 %all-gather.5.cloned.1.call-start = ((), (), s32[]{:S(2)}) async-start(), calls=%async_computation.3 | async-start | bytes 4718592 | tf_op jit(solution)/shard_map/all_gather | solution.py:139
  8.7 563.7 %reduce-scatter.7.cloned.1.call-start = ((), (), s32[]{:S(2)}) async-start(), calls=%async_computation.5 | async-start | bytes 10321920
  9.4 143.3 %copy-start.67 = (f32[32]{0:T(128)}, f32[32]{0:T(128)S(1)}, u32[]{:S(2)}) copy-start(f32[32]{0:T(128)S(1)} %exp.120) | copy-start | bytes 388
  12.5 149.3 %copy-start.34 = (f32[2304]{0:T(1024)}, f32[2304]{0:T(1024)S(1)}, u32[]{:S(2)}) copy-start(f32[2304]{0:T(1024)S(1)} %get-tuple-element.450) | copy-start | bytes 27652
  12.5 149.3 %copy-start.36 = (f32[2304]{0:T(1024)}, f32[2304]{0:T(1024)S(1)}, u32[]{:S(2)}) copy-start(f32[2304]{0:T(1024)S(1)} %get-tuple-element.451) | copy-start | bytes 27652
  12.5 149.3 %copy-start.38 = (f32[2304]{0:T(1024)}, f32[2304]{0:T(1024)S(1)}, u32[]{:S(2)}) copy-start(f32[2304]{0:T(1024)S(1)} %get-tuple-element.452) | copy-start | bytes 27652
  12.5 149.3 %copy-start.40 = (f32[2304]{0:T(1024)}, f32[2304]{0:T(1024)S(1)}, u32[]{:S(2)}) copy-start(f32[2304]{0:T(1024)S(1)} %get-tuple-element.453) | copy-start | bytes 27652
  13.8 137.4 %copy-start.63 = (f32[256]{0:T(256)}, f32[256]{0:T(256)S(1)}, u32[]{:S(2)}) copy-start(f32[256]{0:T(256)S(1)} %add_rsqrt_fusion) | copy-start | bytes 3076
  13.8 139.5 %copy-start.58 = (f32[32]{0:T(128)S(1)}, f32[32]{0:T(128)}, u32[]{:S(2)}) copy-start(f32[32]{0:T(128)} %param.20) | copy-start | bytes 388
  151.2 9.0 %collective-permute-start.2 = (bf16[3,2304]{1,0:T(4,128)(2,1)S(1)}, bf16[3,2304]{1,0:T(4,128)(2,1)S(1)}, u32[]{:S(2)}, u32[]{:S(2)}) collective-permute-start(bf16[3,2304]{1,0:T(4,128)(2,1)S(1)} %slice.123), channel_id=1, source_target_pairs={{0,8},{8,16},{16,24},{1,9},{9,17},{17,25},{2,10},{10,18},{18,26},{... | collective-permute-start | bytes 41480 | tf_op jit(solution)/shard_map/ppermute | solution.py:15
  179.6 6.3 collective-permute-start
  188.3 13.9 %collective-permute-start = (f32[32,64,128]{2,1,0:T(8,128)}, f32[32,64,128]{2,1,0:T(8,128)S(1)}, u32[]{:S(2)}, u32[]{:S(2)}) collective-permute-start(f32[32,64,128]{2,1,0:T(8,128)} %multiply_add_fusion.7), channel_id=1, source_target_pairs={{0,8},{8,16},{16,24},{1,9},{9,17},{17,25},{2,10},{10,18},{18,26},{... | collective-permute-start | bytes 3145736 | tf_op jit(solution)/shard_map/while/body/eval_jaxpr/ppermute | solution.py:15
  204.6 16.3 %collective-permute-start = (f32[32,64,128]{2,1,0:T(8,128)}, f32[32,64,128]{2,1,0:T(8,128)S(1)}, u32[]{:S(2)}, u32[]{:S(2)}) collective-permute-start(f32[32,64,128]{2,1,0:T(8,128)} %multiply_add_fusion.7), channel_id=1, source_target_pairs={{0,8},{8,16},{16,24},{1,9},{9,17},{17,25},{2,10},{10,18},{18,26},{... | collective-permute-start | bytes 3145736 | tf_op jit(solution)/shard_map/while/body/eval_jaxpr/ppermute | solution.py:15
  220.9 14.9 %copy-start.46 = (f32[32]{0:T(128)}, f32[32]{0:T(128)S(1)}, u32[]{:S(2)}) copy-start(f32[32]{0:T(128)S(1)} %get-tuple-element.627) | copy-start | bytes 388
  223.9 11.9 %copy-start.17 = (f32[256,32,64]{0,2,1:T(8,128)}, f32[256,32,64]{0,2,1:T(8,128)S(1)}, u32[]{:S(2)}) copy-start(f32[256,32,64]{0,2,1:T(8,128)S(1)} %fusion.78) | copy-start | bytes 6291460
  267.6 15.6 %collective-permute-start.1 = (bf16[32,64,128]{2,1,0:T(8,128)(2,1)}, bf16[32,64,128]{2,1,0:T(8,128)(2,1)}, u32[]{:S(2)}, u32[]{:S(2)}) collective-permute-start(bf16[32,64,128]{2,1,0:T(8,128)(2,1)} %fusion.132), channel_id=1, source_target_pairs={{8,0},{16,8},{24,16},{9,1},{17,9},{25,17},{10,2},{18,10},{26,18},{... | collective-permute-start | bytes 1572872 | tf_op jit(solution)/shard_map/while/body/eval_jaxpr/ppermute | solution.py:15
  287.9 11.4 %collective-permute-start.1 = (bf16[32,64,128]{2,1,0:T(8,128)(2,1)}, bf16[32,64,128]{2,1,0:T(8,128)(2,1)}, u32[]{:S(2)}, u32[]{:S(2)}) collective-permute-start(bf16[32,64,128]{2,1,0:T(8,128)(2,1)} %fusion.132), channel_id=1, source_target_pairs={{8,0},{16,8},{24,16},{9,1},{17,9},{25,17},{10,2},{18,10},{26,18},{... | collective-permute-start | bytes 1572872 | tf_op jit(solution)/shard_map/while/body/eval_jaxpr/ppermute | solution.py:15
  304.0 10.8 %collective-permute-start.1 = (bf16[32,64,128]{2,1,0:T(8,128)(2,1)}, bf16[32,64,128]{2,1,0:T(8,128)(2,1)}, u32[]{:S(2)}, u32[]{:S(2)}) collective-permute-start(bf16[32,64,128]{2,1,0:T(8,128)(2,1)} %fusion.132), channel_id=1, source_target_pairs={{8,0},{16,8},{24,16},{9,1},{17,9},{25,17},{10,2},{18,10},{26,18},{... | collective-permute-start | bytes 1572872 | tf_op jit(solution)/shard_map/while/body/eval_jaxpr/ppermute | solution.py:15
  361.5 8.2 %copy-start.15 = (f32[256,2304]{1,0:T(8,128)S(1)}, f32[256,2304]{1,0:T(8,128)}, u32[]{:S(2)}) copy-start(f32[256,2304]{1,0:T(8,128)} %get-tuple-element.494) | copy-start | bytes 7077892
  361.5 8.2 %copy-start.18 = (f32[256,2048]{1,0:T(8,128)S(1)}, f32[256,2048]{1,0:T(8,128)}, u32[]{:S(2)}) copy-start(f32[256,2048]{1,0:T(8,128)} %get-tuple-element.506) | copy-start | bytes 6291460
  377.8 7.0 copy-start.68
  383.4 9.9 %copy-start.6 = (f32[256,2304]{1,0:T(8,128)S(1)}, f32[256,2304]{1,0:T(8,128)}, u32[]{:S(2)}) copy-start(f32[256,2304]{1,0:T(8,128)} %copy-done.5) | copy-start | bytes 7077892
  383.4 9.9 %collective-permute-start.3 = (f32[3,2304]{1,0:T(4,128)S(1)}, f32[3,2304]{1,0:T(4,128)S(1)}, u32[]{:S(2)}, u32[]{:S(2)}) collective-permute-start(f32[3,2304]{1,0:T(4,128)S(1)} %pad_add_fusion.1), channel_id=1, source_target_pairs={{8,0},{16,8},{24,16},{9,1},{17,9},{25,17},{10,2},{18,10},{26,18},{... | collective-permute-start | bytes 82952 | tf_op jit(solution)/shard_map/ppermute | solution.py:15
  387.5 6.8 copy-start.24
  412.3 251.1 %reduce-scatter.5.cloned.1.call-start = ((), (), s32[]{:S(2)}) async-start(), calls=%async_computation.4 | async-start | bytes 4718592 | tf_op jit(solution)/shard_map/reduce_scatter | solution.py:203
  417.5 303.6 %all-reduce.18.cloned.1.call-start = ((), (), s32[]{:S(2)}) async-start(), calls=%async_computation.6 | async-start | bytes 3293184 | tf_op jit(solution)/shard_map/psum | solution.py:207
  423.1 240.3 %copy-start.23 = (bf16[1,256,1024]{2,1,0:T(8,128)(2,1)S(1)}, bf16[1,256,1024]{2,1,0:T(8,128)(2,1)}, u32[]{:S(2)}) copy-start(bf16[1,256,1024]{2,1,0:T(8,128)(2,1)} %param.15) | copy-start | bytes 1572868
  423.1 240.3 %copy-start.25 = (bf16[253,2304]{1,0:T(8,128)(2,1)S(1)}, bf16[253,2304]{1,0:T(8,128)(2,1)}, u32[]{:S(2)}) copy-start(bf16[253,2304]{1,0:T(8,128)(2,1)} %copy-done.24) | copy-start | bytes 3497476
  663.4 7.6 %copy-start.55 = (f32[2048]{0:T(1024)S(1)}, f32[2048]{0:T(1024)}, u32[]{:S(2)}) copy-start(f32[2048]{0:T(1024)} %get-tuple-element.445) | copy-start | bytes 24580
  (52 other events, 180.5 us)
Sparse Core Ops, SparseCore 0:
  10.1 134.8 all-gather.2
  147.1 70.9 all-gather.4
  412.4 159.9 reduce-scatter.6
  575.9 87.3 reduce-scatter.4
  666.2 43.9 all-reduce.17
